TPU v7x, 32 devices: a whole 2x2x4 slice. The times are simulated.
32 devices in a mesh: row: 4 (over y, x), col: 8 (over z, core).
Axes of the slice: x: 2, y: 2, z: 4, core: 2. Of those that a mesh axis runs over, the one named last changes fastest.
Arguments:
- boundary_start: float32 [16384, 128], P('row'), may hold values from -6 to 6
- volume_start: float32 [256, 512, 128], P(('row', 'col')), may hold values from -6 to 6
- diag_part: float32 [16384], P(('row', 'col')), may hold values from 1 to 2
- incident: float32 [16384, 128], P(('row', 'col')), may hold values from -6 to 6
- kernel: float32 [16384, 16384], P('row', 'col'), may hold values from -0.015625 to 0.015625
- elem_mats: float32 [256, 512, 512], P(('row', 'col')), may hold values from -0.078125 to 0.078125
- trace_owner: int32 [16384, 1], replicated, may hold values from 0 to 31; in each aligned block of 512 rows (0 to 511, 512 to 1023, ...) at most 32 rows name the same one
- trace_slot: int32 [16384], replicated, may hold values from 0 to 4095
- return_owner: int32 [16384, 1], replicated, may hold values from 0 to 31; in each aligned block of 512 rows (0 to 511, 512 to 1023, ...) at most 32 rows name the same one
- return_slot: int32 [16384], replicated, may hold values from 0 to 4095
- face_match: int32 [256, 64], P(('row', 'col')), may hold values from 0 to 63, each once within a row
Outputs:
- boundary_final: float32 [16384, 128], P('row')
- volume_final: float32 [256, 512, 128], P(('row', 'col'))
Inputs may be any that keep to these rules, and one draw needn't show every extreme that they name: `trace_owner`: in each aligned block of 512 boundary rows (the rows of one device), no device is named more than 32 times; some device is named exactly 32 times in some block. `return_owner`: in each aligned block of 512 boundary rows (the rows of one device), no device is named more than 32 times; some device is named exactly 32 times in some block. `face_match`: each row is a permutation of 0 to 63.
All inputs are finite; a program needn't handle non-finite values.
Results may differ from a plain program's by a relative error of at most 0.0001.
Values sent between devices are 32-bit elements; how exact they have to be, the bound alone decides.
A program may use at most 128 MiB of HBM per device.

v0:
```python
import jax
import jax.numpy as jnp
from jax import lax
from jax.sharding import PartitionSpec as P

ITERS = 3
boundary_step = 0.5
volume_step = 0.6
face_weight = 0.5


def passed_along(block, axis, distance):
    devices = range(lax.axis_size(axis))
    route = [(i - distance, i) for i in devices if i - distance in devices]
    return lax.ppermute(block, axis, route)


def spread(block, axis, holder):
    block = jnp.where(lax.axis_index(axis) == holder, block, jnp.zeros_like(block))
    return lax.psum(block, axis)


def slot_rank(owners):
    row_total = owners.shape[0]
    same_owner = owners[:, None] == owners[None, :]
    positions = jnp.arange(row_total, dtype=jnp.int32)
    earlier = positions[None, :] < positions[:, None]
    return jnp.sum((same_owner & earlier).astype(jnp.int32), axis=1)


def send_plan(owners, rank_rows, devices, capacity):
    positions = jnp.arange(owners.shape[0], dtype=jnp.int32)
    targets = jnp.arange(devices, dtype=jnp.int32)
    places = jnp.arange(capacity, dtype=jnp.int32)
    select = (owners[None, None, :] == targets[:, None, None]) & (
        rank_rows[None, None, :] == places[None, :, None]
    )
    index = jnp.sum(jnp.where(select, positions[None, None, :], 0), axis=2)
    valid_slot = jnp.any(select, axis=2)
    return (index, valid_slot)


def block_plan(owner_blocks, slot_blocks, device_self, capacity):
    mine_rows = owner_blocks == device_self
    rank_rows = jnp.cumsum(mine_rows.astype(jnp.int32), axis=1) - 1
    places = jnp.arange(capacity, dtype=jnp.int32)
    select = mine_rows[:, None, :] & (rank_rows[:, None, :] == places[None, :, None])
    index = jnp.sum(jnp.where(select, slot_blocks[:, None, :], 0), axis=2)
    valid_slot = jnp.any(select, axis=2)
    return (index, valid_slot)


def shards(
    boundary_start,
    volume_start,
    diag_part,
    incident,
    kernel,
    elem_mats,
    trace_owner,
    trace_slot,
    return_owner,
    return_slot,
    face_match,
):
    highest = lax.Precision.HIGHEST
    devices = lax.axis_size(("row", "col"))
    row_devices = lax.axis_size("row")
    col_devices = lax.axis_size("col")
    device_self = lax.axis_index(("row", "col"))
    col_index = lax.axis_index("col")
    total_rows = trace_slot.shape[0]
    share_rows = total_rows // devices
    capacity = max(2, 2 * share_rows // devices)
    panel_length = total_rows // col_devices
    per_panel = col_devices // row_devices
    elem_count, node_count, columns = volume_start.shape
    face_count = face_match.shape[1]
    trace_blocks = trace_owner[:, 0].reshape(devices, share_rows)
    trace_slots = trace_slot.reshape(devices, share_rows)
    return_blocks = return_owner[:, 0].reshape(devices, share_rows)
    return_slots = return_slot.reshape(devices, share_rows)
    trace_send, trace_send_ok = block_plan(trace_blocks, trace_slots, device_self, capacity)
    own_trace = lax.dynamic_index_in_dim(trace_blocks, device_self, 0, keepdims=False)
    trace_pick = own_trace * capacity + slot_rank(own_trace)
    own_return = lax.dynamic_index_in_dim(return_blocks, device_self, 0, keepdims=False)
    flux_send, flux_send_ok = send_plan(own_return, slot_rank(own_return), devices, capacity)
    flux_take, flux_take_ok = block_plan(return_blocks, return_slots, device_self, capacity)
    panel_current = boundary_start
    volume_field = volume_start
    for sweep_index in range(ITERS):
        share_current = lax.dynamic_slice_in_dim(
            panel_current, col_index * share_rows, share_rows, 0
        )
        volume_flat = volume_field.reshape(elem_count * node_count, columns)
        outgoing = jnp.where(trace_send_ok[:, :, None], volume_flat[trace_send], 0.0)
        arrived = lax.all_to_all(outgoing, ("row", "col"), split_axis=0, concat_axis=0, tiled=True)
        traced = arrived.reshape(devices * capacity, columns)[trace_pick]
        leaving = jnp.where(flux_send_ok[:, :, None], share_current[flux_send], 0.0)
        landed = lax.all_to_all(leaving, ("row", "col"), split_axis=0, concat_axis=0, tiled=True)
        landed_rows = jnp.where(flux_take_ok[:, :, None], landed, 0.0).reshape(
            devices * capacity, columns
        )
        flux_field = (
            jnp.zeros_like(volume_flat)
            .at[flux_take.reshape(-1)]
            .add(landed_rows)
            .reshape(volume_field.shape)
        )
        lower_faces = passed_along(volume_field[:, node_count - face_count :, :], ("row", "col"), 1)
        matched = jax.vmap(lambda face_rows, face_order: face_rows[face_order])(
            lower_faces, face_match
        )
        half_panel = lax.dynamic_slice_in_dim(
            panel_current, col_index % per_panel * panel_length, panel_length, 0
        )
        column_values = spread(half_panel, "row", col_index // per_panel)
        local_term = diag_part[:, None] * share_current - incident - traced
        partial_value = jnp.dot(
            kernel, column_values, precision=highest, preferred_element_type=jnp.float32
        )
        row_start = col_index * share_rows
        own_part = lax.dynamic_slice_in_dim(partial_value, row_start, share_rows, 0) + local_term
        partial_value = lax.dynamic_update_slice_in_dim(partial_value, own_part, row_start, 0)
        residual = lax.psum(partial_value, "col")
        panel_current = panel_current - boundary_step * residual
        applied = jnp.einsum("enm,emr->enr", elem_mats, volume_field, precision=highest)
        updated = volume_field - volume_step * (volume_field + applied - flux_field)
        volume_field = updated.at[:, :face_count, :].add(volume_step * face_weight * matched)
    return (panel_current, volume_field)


def solution(mesh):
    placed = (
        P("row", None),
        P(("row", "col"), None, None),
        P(("row", "col")),
        P(("row", "col"), None),
        P("row", "col"),
        P(("row", "col"), None, None),
        P(),
        P(),
        P(),
        P(),
        P(("row", "col"), None),
    )
    return jax.shard_map(
        shards,
        mesh=mesh,
        in_specs=placed,
        out_specs=(P("row", None), P(("row", "col"), None, None)),
        check_vma=False,
    )
```

profile of v0, /device:TPU:0, one launch (start us, length us, event | category | flops | bytes accessed | tf_op | source)
XLA Modules:
  0.0 601.1 jit_solution(13699476681869330466)
XLA Ops:
  7.2 2.9 copy.59
  10.1 2.4 dynamic-slice_select_fusion.2
  12.8 1.2 reduce-window.14
  17.0 2.8 gather_fusion
  19.9 1.0 broadcast_select_fusion.8
  20.9 7.3 %all-to-all-start = ((f32[32,32,128]{2,1,0:T(8,128)}), f32[32,32,128]{2,1,0:T(8,128)S(1)}, u32[]{:S(2)}, u32[]{:S(2)}) async-start(f32[32,32,128]{2,1,0:T(8,128)} %broadcast_select_fusion.8), calls=%async_computation | async-start | bytes 1048576 | tf_op jit(solution)/shard_map/all_to_all | solution.py:97
  28.9 2.7 collective-permute-start
  33.9 1.2 reduce-window.16
  36.1 8.7 %all-to-all-done = f32[32,32,128]{2,1,0:T(8,128)S(1)} async-done(((f32[32,32,128]{2,1,0:T(8,128)}), f32[32,32,128]{2,1,0:T(8,128)S(1)}, u32[]{:S(2)}, u32[]{:S(2)}) %all-to-all-start) | async-done | bytes 524320 | tf_op jit(solution)/shard_map/all_to_all | solution.py:97
  44.8 1.0 gather_fusion.1
  46.0 23.2 %all-reduce.7.cloned.1.call-done = f32[2048,128]{0,1:T(8,128)} async-done(((f32[2048,128]{0,1:T(8,128)}), f32[2048,128]{0,1:T(8,128)}) %all-reduce.7.cloned.1.call-update) | async-done | bytes 1048592 | tf_op jit(solution)/shard_map/psum | solution.py:20
  69.2 38.4 %fusion.29 = f32[128,4096]{1,0:T(8,128)S(1)} fusion(f32[2048,128]{0,1:T(8,128)} %all-reduce.7.cloned.1.call-done, f32[4096,2048]{1,0:T(8,128)} %param.21), kind=kOutput, calls=%fused_computation.106 | convolution fusion | flops 12884901888 | bytes 36700160 | tf_op jit(solution)/shard_map/dot_general | solution.py:119
  108.3 1.0 constant_dynamic-slice_fusion.4
  109.3 1.3 copy-done.5
  110.8 2.8 gather_fusion.2
  114.6 4.6 all-to-all-start.1
  120.9 3.7 gather_fusion.9
  124.7 10.8 %all-to-all-done.1 = f32[32,32,128]{2,1,0:T(8,128)S(1)} async-done(((f32[32,32,128]{2,1,0:T(8,128)}), f32[32,32,128]{2,1,0:T(8,128)S(1)}, u32[]{:S(2)}, u32[]{:S(2)}) %all-to-all-start.1) | async-done | bytes 524320 | tf_op jit(solution)/shard_map/all_to_all | solution.py:100
  135.7 8.0 %scatter_custom_fusion = f32[4096,128]{1,0:T(8,128)} fusion(s32[1024]{0:T(1024)S(1)} %bitcast.132, f32[1024,128]{1,0:T(8,128)S(1)} %bitcast.123, f32[]{:T(128)} %constant.143.clone.1), kind=kCustom, calls=%fused_computation.44 | custom fusion | flops 131072 | bytes 2097156 | tf_op jit(solution)/shard_map/scatter-add | solution.py:107
  143.7 11.2 %multiply_subtract_fusion.2 = f32[8,512,128]{2,1,0:T(8,128)S(1)} fusion(f32[8,512,128]{2,1,0:T(8,128)} %param.18, f32[8,512,128]{2,1,0:T(8,128)} %bitcast.112, f32[8,512,512]{2,1,0:T(8,128)} %param.22), kind=kOutput, calls=%fused_computation.28 | convolution fusion | flops 3223322624 | bytes 14680064 | tf_op jit(solution)/shard_map/enm,emr->enr/dot_general | solution.py:127
  155.0 2.8 gather_fusion.3
  157.8 33.4 %all-reduce.9.cloned.1.call-done = f32[4096,128]{0,1:T(8,128)} async-done(((f32[4096,128]{0,1:T(8,128)}), f32[4096,128]{0,1:T(8,128)}) %all-reduce.9.cloned.1.call-update) | async-done | bytes 2097168 | tf_op jit(solution)/shard_map/psum | solution.py:125
  191.2 2.5 multiply_subtract_fusion.3
  193.7 1.3 copy-done.3
  195.0 1.0 dynamic-slice_select_fusion.1
  196.2 20.6 %all_to_all.30 = f32[32,32,128]{2,1,0:T(8,128)S(1)} all-to-all(f32[32,32,128]{2,1,0:T(8,128)S(1)} %broadcast_select_fusion.5), channel_id=1, replica_groups=mesh['row'=4,'col'=8] {'row','col'}, dimensions={0} | all-to-all | bytes 1048576 | tf_op jit(solution)/shard_map/all_to_all | solution.py:97
  216.9 1.0 gather_fusion.4
  218.1 35.8 %all-reduce.11.cloned.1.call-done = f32[2048,128]{0,1:T(8,128)} async-done(((f32[2048,128]{0,1:T(8,128)}), f32[2048,128]{0,1:T(8,128)}) %all-reduce.11.cloned.1.call-update) | async-done | bytes 1048592 | tf_op jit(solution)/shard_map/psum | solution.py:20
  253.9 39.2 %fusion.30 = f32[128,4096]{1,0:T(8,128)} fusion(f32[2048,128]{0,1:T(8,128)} %all-reduce.11.cloned.1.call-done, f32[4096,2048]{1,0:T(8,128)} %param.21), kind=kOutput, calls=%fused_computation.107 | convolution fusion | flops 12884901888 | bytes 36700160 | tf_op jit(solution)/shard_map/dot_general | solution.py:119
  293.0 1.6 copy.87
  294.6 1.1 constant_dynamic-slice_fusion.2
  295.8 1.3 copy-done.6
  297.2 2.8 gather_fusion.5
  301.0 4.6 all-to-all-start.3
  305.7 2.2 collective-permute-start.1
  307.9 1.1 collective-permute-done.1
  309.0 3.7 gather_fusion.10
  312.8 9.4 %all-to-all-done.3 = f32[32,32,128]{2,1,0:T(8,128)S(1)} async-done(((f32[32,32,128]{2,1,0:T(8,128)}), f32[32,32,128]{2,1,0:T(8,128)S(1)}, u32[]{:S(2)}, u32[]{:S(2)}) %all-to-all-start.3) | async-done | bytes 524320 | tf_op jit(solution)/shard_map/all_to_all | solution.py:100
  322.4 8.1 %scatter_custom_fusion.1 = f32[4096,128]{1,0:T(8,128)} fusion(s32[1024]{0:T(1024)S(1)} %bitcast.133, f32[1024,128]{1,0:T(8,128)S(1)} %bitcast.124, f32[]{:T(128)} %constant.143.clone.1), kind=kCustom, calls=%fused_computation.42 | custom fusion | flops 131072 | bytes 2097156 | tf_op jit(solution)/shard_map/scatter-add | solution.py:107
  330.6 10.9 %fusion.6 = f32[8,512,128]{2,1,0:T(8,128)S(1)} fusion(f32[8,512,128]{2,1,0:T(8,128)} %copy-done, f32[8,512,128]{2,1,0:T(8,128)} %bitcast.111, f32[8,512,512]{2,1,0:T(8,128)} %param.22), kind=kOutput, calls=%fused_computation.25 | convolution fusion | flops 3223322624 | bytes 14680064 | tf_op jit(solution)/shard_map/enm,emr->enr/dot_general | solution.py:127
  341.5 2.8 gather_fusion.6
  344.4 46.2 %all-reduce.13.cloned.1.call-done = f32[4096,128]{0,1:T(8,128)} async-done(((f32[4096,128]{0,1:T(8,128)}), f32[4096,128]{0,1:T(8,128)}) %all-reduce.13.cloned.1.call-update) | async-done | bytes 2097168 | tf_op jit(solution)/shard_map/psum | solution.py:125
  390.5 2.5 multiply_subtract_fusion.1
  393.0 1.3 copy-done.2
  394.3 1.0 dynamic-slice_select_fusion
  395.6 20.3 %all_to_all.31 = f32[32,32,128]{2,1,0:T(8,128)S(1)} all-to-all(f32[32,32,128]{2,1,0:T(8,128)S(1)} %broadcast_select_fusion.2), channel_id=1, replica_groups=mesh['row'=4,'col'=8] {'row','col'}, dimensions={0} | all-to-all | bytes 1048576 | tf_op jit(solution)/shard_map/all_to_all | solution.py:97
  415.8 1.0 gather_fusion.7
  417.0 36.1 %all-reduce.15.cloned.1.call-done = f32[2048,128]{0,1:T(8,128)} async-done(((f32[2048,128]{0,1:T(8,128)}), f32[2048,128]{0,1:T(8,128)}) %all-reduce.15.cloned.1.call-update) | async-done | bytes 1048592 | tf_op jit(solution)/shard_map/psum | solution.py:20
  453.1 39.1 %fusion.31 = f32[128,4096]{1,0:T(8,128)} fusion(f32[2048,128]{0,1:T(8,128)} %all-reduce.15.cloned.1.call-done, f32[4096,2048]{1,0:T(8,128)} %param.21), kind=kOutput, calls=%fused_computation.108 | convolution fusion | flops 12884901888 | bytes 36700160 | tf_op jit(solution)/shard_map/dot_general | solution.py:119
  492.2 1.6 copy.91
  493.8 1.1 constant_dynamic-slice_fusion
  495.0 1.3 copy-done.4
  496.4 2.8 gather_fusion.8
  500.2 4.6 all-to-all-start.5
  504.9 2.2 collective-permute-start.2
  507.1 1.1 collective-permute-done.2
  508.2 3.7 gather_fusion.11
  511.9 9.5 %all-to-all-done.5 = f32[32,32,128]{2,1,0:T(8,128)S(1)} async-done(((f32[32,32,128]{2,1,0:T(8,128)}), f32[32,32,128]{2,1,0:T(8,128)S(1)}, u32[]{:S(2)}, u32[]{:S(2)}) %all-to-all-start.5) | async-done | bytes 524320 | tf_op jit(solution)/shard_map/all_to_all | solution.py:100
  521.6 8.2 %scatter_custom_fusion.2 = f32[4096,128]{1,0:T(8,128)} fusion(s32[1024]{0:T(1024)S(1)} %bitcast.134, f32[1024,128]{1,0:T(8,128)S(1)} %bitcast.122, f32[]{:T(128)} %constant.143.clone.1), kind=kCustom, calls=%fused_computation.40 | custom fusion | flops 131072 | bytes 2097156 | tf_op jit(solution)/shard_map/scatter-add | solution.py:107
  529.8 10.7 %fusion.3 = f32[8,512,128]{2,1,0:T(8,128)} fusion(f32[8,512,128]{2,1,0:T(8,128)S(1)} %fusion.20, f32[8,512,128]{2,1,0:T(8,128)} %bitcast.110, f32[8,512,512]{2,1,0:T(8,128)} %param.22), kind=kOutput, calls=%fused_computation.21 | convolution fusion | flops 3223322624 | bytes 14680064 | tf_op jit(solution)/shard_map/enm,emr->enr/dot_general | solution.py:127
  540.5 1.7 fusion.19
  542.2 47.5 %all-reduce.17.cloned.1.call-done = f32[4096,128]{0,1:T(8,128)} async-done(((f32[4096,128]{0,1:T(8,128)}), f32[4096,128]{0,1:T(8,128)}) %all-reduce.17.cloned.1.call-update) | async-done | bytes 2097168 | tf_op jit(solution)/shard_map/psum | solution.py:125
  589.7 2.4 multiply_subtract_fusion
  592.2 1.8 copy.73
  (103 shorter events, 14.7 us)
Async XLA Ops:
  7.2 62.0 %all-reduce.7.cloned.1.call-start = ((), (), s32[]{:S(2)}) async-start(), calls=%async_computation.6 | async-start | bytes 2097152 | tf_op jit(solution)/shard_map/psum | solution.py:20
  10.1 2.5 copy-start.8
  10.1 2.5 copy-start.9
  10.1 5.5 copy-start.10
  10.1 6.9 %copy-start.1 = (f32[8,512,128]{2,1,0:T(8,128)S(1)}, f32[8,512,128]{2,1,0:T(8,128)}, u32[]{:S(2)}) copy-start(f32[8,512,128]{2,1,0:T(8,128)} %param.18) | copy-start | bytes 6291460
  19.8 13.8 %copy-start.7 = (f32[512,128]{1,0:T(8,128)S(1)}, f32[512,128]{1,0:T(8,128)}, u32[]{:S(2)}) copy-start(f32[512,128]{1,0:T(8,128)} %param.20) | copy-start | bytes 786436
  19.8 15.4 %copy-start.11 = (s32[16384]{0:T(1024)S(1)}, s32[16384]{0:T(1024)}, u32[]{:S(2)}) copy-start(s32[16384]{0:T(1024)} %param.26) | copy-start | bytes 196612
  20.9 23.9 %all-to-all-start = ((f32[32,32,128]{2,1,0:T(8,128)}), f32[32,32,128]{2,1,0:T(8,128)S(1)}, u32[]{:S(2)}, u32[]{:S(2)}) async-start(f32[32,32,128]{2,1,0:T(8,128)} %broadcast_select_fusion.8), calls=%async_computation | async-start | bytes 1048576 | tf_op jit(solution)/shard_map/all_to_all | solution.py:97
  28.9 92.0 %collective-permute-start = (f32[8,64,128]{2,1,0:T(8,128)}, f32[8,64,128]{2,1,0:T(8,128)S(1)}, u32[]{:S(2)}, u32[]{:S(2)}) collective-permute-start(f32[8,64,128]{2,1,0:T(8,128)} %slice.98), channel_id=1, source_target_pairs={{0,1},{1,2},{2,3},{3,4},{4,5},{5,6},{6,7},{7,8},{8,9},{9,10},{10,1... | collective-permute-start | bytes 786440 | tf_op jit(solution)/shard_map/ppermute | solution.py:15
  107.6 0.7 copy-start.12
  109.3 1.3 copy-start.5
  113.6 6.5 %copy-start.13 = (s32[8,64]{1,0:T(8,128)S(1)}, s32[8,64]{1,0:T(8,128)}, u32[]{:S(2)}) copy-start(s32[8,64]{1,0:T(8,128)} %param.27) | copy-start | bytes 6148
  114.6 20.9 %all-to-all-start.1 = ((f32[32,32,128]{2,1,0:T(8,128)}), f32[32,32,128]{2,1,0:T(8,128)S(1)}, u32[]{:S(2)}, u32[]{:S(2)}) async-start(f32[32,32,128]{2,1,0:T(8,128)} %broadcast_select_fusion.7), calls=%async_computation.1 | async-start | bytes 1048576 | tf_op jit(solution)/shard_map/all_to_all | solution.py:100
  119.2 72.0 %all-reduce.9.cloned.1.call-start = ((), (), s32[]{:S(2)}) async-start(), calls=%async_computation.7 | async-start | bytes 4194304 | tf_op jit(solution)/shard_map/psum | solution.py:125
  124.6 129.2 %all-reduce.11.cloned.1.call-start = ((), (), s32[]{:S(2)}) async-start(), calls=%async_computation.8 | async-start | bytes 2097152 | tf_op jit(solution)/shard_map/psum | solution.py:20
  155.0 150.7 %copy-start = (f32[8,512,128]{2,1,0:T(8,128)}, f32[8,512,128]{2,1,0:T(8,128)S(1)}, u32[]{:S(2)}) copy-start(f32[8,512,128]{2,1,0:T(8,128)S(1)} %fusion.21) | copy-start | bytes 6291460
  193.6 1.3 copy-start.3
  295.8 1.3 copy-start.6
  301.0 21.2 %all-to-all-start.3 = ((f32[32,32,128]{2,1,0:T(8,128)}), f32[32,32,128]{2,1,0:T(8,128)S(1)}, u32[]{:S(2)}, u32[]{:S(2)}) async-start(f32[32,32,128]{2,1,0:T(8,128)} %broadcast_select_fusion.4), calls=%async_computation.3 | async-start | bytes 1048576 | tf_op jit(solution)/shard_map/all_to_all | solution.py:100
  305.6 84.9 %all-reduce.13.cloned.1.call-start = ((), (), s32[]{:S(2)}) async-start(), calls=%async_computation.9 | async-start | bytes 4194304 | tf_op jit(solution)/shard_map/psum | solution.py:125
  305.7 3.3 collective-permute-start.1
  312.7 140.4 %all-reduce.15.cloned.1.call-start = ((), (), s32[]{:S(2)}) async-start(), calls=%async_computation.10 | async-start | bytes 2097152 | tf_op jit(solution)/shard_map/psum | solution.py:20
  393.0 1.3 copy-start.2
  495.0 1.3 copy-start.4
  500.2 21.2 %all-to-all-start.5 = ((f32[32,32,128]{2,1,0:T(8,128)}), f32[32,32,128]{2,1,0:T(8,128)S(1)}, u32[]{:S(2)}, u32[]{:S(2)}) async-start(f32[32,32,128]{2,1,0:T(8,128)} %broadcast_select_fusion.1), calls=%async_computation.5 | async-start | bytes 1048576 | tf_op jit(solution)/shard_map/all_to_all | solution.py:100
  504.8 84.9 %all-reduce.17.cloned.1.call-start = ((), (), s32[]{:S(2)}) async-start(), calls=%async_computation.11 | async-start | bytes 4194304 | tf_op jit(solution)/shard_map/psum | solution.py:125
  504.9 3.3 collective-permute-start.2
Sparse Core Ops, SparseCore 0:
  12.7 56.4 all-reduce.6
  124.8 66.3 all-reduce.8
  196.2 57.6 all-reduce.10
  312.9 77.6 all-reduce.12
  395.5 57.5 all-reduce.14
  512.0 77.6 all-reduce.16
where the time goes:
time: 605 us; the launch traced here: 601 us
  waiting for transfers between devices  263 us (43%)
  matrix products  150 us (25%)
  other arithmetic  55 us (9%)
  local copies, waits for them, and re-layouts  49 us (8%)
  blocking collectives  40.9 us (7%)
  starting transfers between devices  28.6 us (5%)
  between operations  15.1 us (2%)
    psum x3, waiting for transfers between devices, shards(): residual = lax.psum(partial_value, 'col')  127 us
    dot_general x3, matrix products, shards(): jnp.dot(kernel, column_values, precision=highest, preferred_element_type=...  117 us
    psum x3, waiting for transfers between devices, spread(): return lax.psum(block, axis)  95.1 us
    all_to_all x2, blocking collectives, shards(): lax.all_to_all(outgoing, ('row', 'col'), split_axis=0, concat_axis=0, til...  40.9 us
    dot_general x3, matrix products, shards(): jnp.einsum('enm,emr->enr', elem_mats, volume_field, precision=highest)  32.8 us
    all_to_all x3, waiting for transfers between devices, shards(): lax.all_to_all(leaving, ('row', 'col'), split_axis=0, concat_axis=0, tile...  29.7 us
    scatter-add x3, other arithmetic, shards(): flux_field = jnp.zeros_like(volume_flat).at[flux_take.reshape(-1)].add(la...  24.3 us
    unnamed x35, local copies, waits for them, and re-layouts  15.8 us
  transfers between devices with their start and end apart: 13, of which 12 were waited for; matrix products, arithmetic and copies ran while one was open for 23% of the time, Pallas kernels for 0%

commit v1 on v0

--- a/solution.py
+++ b/solution.py
@@ -122,7 +122,8 @@
         row_start = col_index * share_rows
         own_part = lax.dynamic_slice_in_dim(partial_value, row_start, share_rows, 0) + local_term
         partial_value = lax.dynamic_update_slice_in_dim(partial_value, own_part, row_start, 0)
-        residual = lax.psum(partial_value, "col")
+        parts = lax.all_gather(partial_value, "col")
+        residual = jnp.sum(parts, axis=0)
         panel_current = panel_current - boundary_step * residual
         applied = jnp.einsum("enm,emr->enr", elem_mats, volume_field, precision=highest)
         updated = volume_field - volume_step * (volume_field + applied - flux_field)

time: 605 us -> 919 us (1.52)
  waiting for transfers between devices: 263 us -> 507 us
  other arithmetic: 55 us -> 88 us
  local copies, waits for them, and re-layouts: 49 us -> 76.6 us
    all_gather x0 -> x3, waiting for transfers between devices: none -> 425 us  [shards(): parts = lax.all_gather(partial_value, 'col')]
    psum x3 -> x0, waiting for transfers between devices: 127 us -> none  [shards(): residual = lax.psum(partial_value, 'col')]
    all_to_all x3 -> x2, waiting for transfers between devices: 29.7 us -> 5.08 us  [shards(): lax.all_to_all(leaving, ('row', 'col'), split_axis=0, concat_axis=0, tile...]
    reduce_sum x0 -> x3, other arithmetic: none -> 24.4 us  [shards(): residual = jnp.sum(parts, axis=0)]
    all_to_all x2 -> x1, blocking collectives: 40.9 us -> 18.8 us  [shards(): lax.all_to_all(outgoing, ('row', 'col'), split_axis=0, concat_axis=0, til...]
    psum x3, waiting for transfers between devices: 95.1 us -> 75.3 us  [spread(): return lax.psum(block, axis)]
    all_to_all x0 -> x1, blocking collectives: none -> 18.8 us  [shards(): lax.all_to_all(leaving, ('row', 'col'), split_axis=0, concat_axis=0, tile...]
    all_to_all x1 -> x2, starting transfers between devices: 7.33 us -> 16.9 us  [shards(): lax.all_to_all(outgoing, ('row', 'col'), split_axis=0, concat_axis=0, til...]
  transfers between devices with their start and end apart: 13 -> 13, of which waited for: 12 -> 8; matrix products, arithmetic and copies ran while one was open for 23% -> 21% of each run, Pallas kernels for 0% -> 0%
where the time goes in v1:
time: 919 us; the launch traced here: 910 us
  waiting for transfers between devices  507 us (55%)
  matrix products  152 us (17%)
  other arithmetic  88 us (10%)
  local copies, waits for them, and re-layouts  76.6 us (8%)
  blocking collectives  37.6 us (4%)
  starting transfers between devices  34.3 us (4%)
  between operations  15.1 us (2%)
    all_gather x3, waiting for transfers between devices, shards(): parts = lax.all_gather(partial_value, 'col')  425 us
    dot_general x3, matrix products, shards(): jnp.dot(kernel, column_values, precision=highest, preferred_element_type=...  117 us
    psum x3, waiting for transfers between devices, spread(): return lax.psum(block, axis)  75.3 us
    dot_general x3, matrix products, shards(): jnp.einsum('enm,emr->enr', elem_mats, volume_field, precision=highest)  34.3 us
    scatter-add x3, other arithmetic, shards(): flux_field = jnp.zeros_like(volume_flat).at[flux_take.reshape(-1)].add(la...  24.5 us
    reduce_sum x3, other arithmetic, shards(): residual = jnp.sum(parts, axis=0)  24.4 us
    unnamed x37, local copies, waits for them, and re-layouts  19.9 us
    all_to_all x1, blocking collectives, shards(): lax.all_to_all(outgoing, ('row', 'col'), split_axis=0, concat_axis=0, til...  18.8 us
  transfers between devices with their start and end apart: 13, of which 8 were waited for; matrix products, arithmetic and copies ran while one was open for 21% of the time, Pallas kernels for 0%

profile of v1, /device:TPU:0, one launch (start us, length us, event | category | flops | bytes accessed | tf_op | source)
XLA Modules:
  0.0 910.1 jit_solution(1967651826180414449)
XLA Ops:
  7.7 1.6 reduce.16
  9.3 1.6 reduce.17
  12.7 1.9 copy.112
  14.6 1.3 copy-done.6
  16.1 2.8 gather_fusion.2
  19.9 7.3 all-to-all-start.1
  28.1 2.3 collective-permute-start
  30.4 2.4 dynamic-slice_select_fusion.2
  40.4 4.0 gather_fusion
  44.4 3.7 gather_fusion.9
  48.4 8.1 scatter_custom_fusion
  56.5 11.2 %multiply_subtract_fusion.2 = f32[8,512,128]{2,1,0:T(8,128)S(1)} fusion(f32[8,512,128]{2,1,0:T(8,128)} %param.18, f32[8,512,128]{2,1,0:T(8,128)} %bitcast.124, f32[8,512,512]{2,1,0:T(8,128)} %param.22), kind=kOutput, calls=%fused_computation.28 | convolution fusion | flops 3223322624 | bytes 14680064 | tf_op jit(solution)/shard_map/enm,emr->enr/dot_general | solution.py:128
  67.8 2.8 gather_fusion.3
  70.6 1.2 broadcast_select_fusion.5
  71.9 5.8 all-to-all-start
  77.7 13.8 %all-reduce.4.cloned.1.call-done = f32[2048,128]{0,1:T(8,128)} async-done(((f32[2048,128]{0,1:T(8,128)}), f32[2048,128]{0,1:T(8,128)}) %all-reduce.4.cloned.1.call-update) | async-done | bytes 1048592 | tf_op jit(solution)/shard_map/psum | solution.py:20
  91.5 39.1 %fusion.26 = f32[128,4096]{1,0:T(8,128)} fusion(f32[2048,128]{0,1:T(8,128)} %all-reduce.4.cloned.1.call-done, f32[4096,2048]{1,0:T(8,128)} %param.21), kind=kOutput, calls=%fused_computation.106 | convolution fusion | flops 12884901888 | bytes 36700160 | tf_op jit(solution)/shard_map/dot_general | solution.py:119
  130.7 3.1 copy.141
  135.0 1.9 bitcast_dynamic-update-slice_fusion.2
  136.9 2.9 copy.110
  140.1 151.4 %all-gather.4.cloned.1.call-done = f32[8,4096,128]{2,1,0:T(8,128)} async-done(((f32[1,4096,128]{2,1,0:T(8,128)}), f32[8,4096,128]{2,1,0:T(8,128)}) %all-gather.4.cloned.1.call-update) | async-done | bytes 16777232 | tf_op jit(solution)/shard_map/all_gather | solution.py:125
  291.4 8.1 reduce_sum.82
  299.6 2.9 copy.111
  302.5 2.5 multiply_subtract_fusion.3
  305.0 1.3 copy-done.5
  307.5 18.8 %all_to_all.30 = f32[32,32,128]{2,1,0:T(8,128)S(1)} all-to-all(f32[32,32,128]{2,1,0:T(8,128)S(1)} %copy-done.8), channel_id=1, replica_groups=mesh['row'=4,'col'=8] {'row','col'}, dimensions={0} | all-to-all | bytes 1048576 | tf_op jit(solution)/shard_map/all_to_all | solution.py:97
  327.5 36.1 %all-reduce.6.cloned.1.call-done = f32[2048,128]{0,1:T(8,128)} async-done(((f32[2048,128]{0,1:T(8,128)}), f32[2048,128]{0,1:T(8,128)}) %all-reduce.6.cloned.1.call-update) | async-done | bytes 1048592 | tf_op jit(solution)/shard_map/psum | solution.py:20
  363.5 39.2 %fusion.27 = f32[128,4096]{1,0:T(8,128)} fusion(f32[2048,128]{0,1:T(8,128)} %all-reduce.6.cloned.1.call-done, f32[4096,2048]{1,0:T(8,128)} %param.21), kind=kOutput, calls=%fused_computation.107 | convolution fusion | flops 12884901888 | bytes 36700160 | tf_op jit(solution)/shard_map/dot_general | solution.py:119
  402.7 3.1 copy.143
  405.8 1.9 bitcast_dynamic-update-slice_fusion.1
  407.7 2.9 copy.118
  411.7 2.8 gather_fusion.5
  414.6 147.3 %all-gather.6.cloned.1.call-done = f32[8,4096,128]{2,1,0:T(8,128)} async-done(((f32[1,4096,128]{2,1,0:T(8,128)}), f32[8,4096,128]{2,1,0:T(8,128)}) %all-gather.6.cloned.1.call-update) | async-done | bytes 16777232 | tf_op jit(solution)/shard_map/all_gather | solution.py:125
  561.8 8.1 reduce_sum.87
  570.0 2.9 copy.119
  572.9 2.5 multiply_subtract_fusion.1
  575.3 1.3 copy-done.2
  576.8 4.0 gather_fusion.8
  580.8 2.0 broadcast_select_fusion.1
  582.9 18.8 %all_to_all.31 = f32[32,32,128]{2,1,0:T(8,128)S(1)} all-to-all(f32[32,32,128]{2,1,0:T(8,128)S(1)} %get-tuple-element.51), channel_id=1, replica_groups=mesh['row'=4,'col'=8] {'row','col'}, dimensions={0} | all-to-all | bytes 1048576 | tf_op jit(solution)/shard_map/all_to_all | solution.py:100
  601.7 3.3 all-to-all-start.5
  605.1 2.1 collective-permute-start.1
  608.4 6.0 gather_fusion.10
  616.5 5.1 all-to-all-done.5
  621.6 2.0 broadcast_select_fusion
  623.6 8.0 scatter_custom_fusion.1
  631.6 11.2 %fusion.6 = f32[8,512,128]{2,1,0:T(8,128)S(1)} fusion(f32[8,512,128]{2,1,0:T(8,128)} %copy-done, f32[8,512,128]{2,1,0:T(8,128)} %bitcast.123, f32[8,512,512]{2,1,0:T(8,128)} %param.22), kind=kOutput, calls=%fused_computation.25 | convolution fusion | flops 3223322624 | bytes 14680064 | tf_op jit(solution)/shard_map/enm,emr->enr/dot_general | solution.py:128
  642.9 2.8 gather_fusion.6
  646.7 11.2 %all-to-all-start.4 = ((f32[32,32,128]{2,1,0:T(8,128)}), f32[32,32,128]{2,1,0:T(8,128)S(1)}, u32[]{:S(2)}, u32[]{:S(2)}) async-start(f32[32,32,128]{2,1,0:T(8,128)} %broadcast_select_fusion.2), calls=%async_computation.4 | async-start | bytes 1048576 | tf_op jit(solution)/shard_map/all_to_all | solution.py:97
  658.1 25.4 %all-reduce.8.cloned.1.call-done = f32[2048,128]{0,1:T(8,128)} async-done(((f32[2048,128]{0,1:T(8,128)}), f32[2048,128]{0,1:T(8,128)}) %all-reduce.8.cloned.1.call-update) | async-done | bytes 1048592 | tf_op jit(solution)/shard_map/psum | solution.py:20
  683.5 39.1 %fusion.28 = f32[128,4096]{1,0:T(8,128)} fusion(f32[2048,128]{0,1:T(8,128)} %all-reduce.8.cloned.1.call-done, f32[4096,2048]{1,0:T(8,128)} %param.21), kind=kOutput, calls=%fused_computation.108 | convolution fusion | flops 12884901888 | bytes 36700160 | tf_op jit(solution)/shard_map/dot_general | solution.py:119
  722.6 3.1 copy.146
  727.0 1.9 bitcast_dynamic-update-slice_fusion
  728.9 2.9 copy.125
  731.8 8.4 scatter_custom_fusion.2
  740.2 1.7 collective-permute-start.2
  741.9 11.9 %fusion.3 = f32[8,512,128]{2,1,0:T(8,128)} fusion(f32[8,512,128]{2,1,0:T(8,128)S(1)} %fusion.20, f32[8,512,128]{2,1,0:T(8,128)} %bitcast.122, f32[8,512,512]{2,1,0:T(8,128)} %param.22), kind=kOutput, calls=%fused_computation.21 | convolution fusion | flops 3223322624 | bytes 14680064 | tf_op jit(solution)/shard_map/enm,emr->enr/dot_general | solution.py:128
  753.8 3.7 gather_fusion.11
  757.4 1.7 fusion.19
  759.1 126.6 %all-gather.8.cloned.1.call-done = f32[8,4096,128]{2,1,0:T(8,128)} async-done(((f32[1,4096,128]{2,1,0:T(8,128)}), f32[8,4096,128]{2,1,0:T(8,128)}) %all-gather.8.cloned.1.call-update) | async-done | bytes 16777232 | tf_op jit(solution)/shard_map/all_gather | solution.py:125
  885.8 8.2 reduce_sum.88
  894.0 3.1 copy.126
  897.0 3.2 multiply_subtract_fusion
  900.2 2.9 copy.130
  (114 shorter events, 22.7 us)
Async XLA Ops:
  14.6 1.3 copy-start.6
  18.9 8.4 copy-start.1
  19.9 28.2 %all-to-all-start.1 = ((f32[32,32,128]{2,1,0:T(8,128)}), f32[32,32,128]{2,1,0:T(8,128)S(1)}, u32[]{:S(2)}, u32[]{:S(2)}) async-start(f32[32,32,128]{2,1,0:T(8,128)} %broadcast_select_fusion.7), calls=%async_computation.1 | async-start | bytes 1048576 | tf_op jit(solution)/shard_map/all_to_all | solution.py:100
  27.3 5.6 copy-start.9
  27.3 5.6 copy-start.10
  27.3 64.2 %all-reduce.4.cloned.1.call-start = ((), (), s32[]{:S(2)}) async-start(), calls=%async_computation.6 | async-start | bytes 2097152 | tf_op jit(solution)/shard_map/psum | solution.py:20
  28.1 6.5 copy-start.11
  28.1 16.4 %collective-permute-start = (f32[8,64,128]{2,1,0:T(8,128)}, f32[8,64,128]{2,1,0:T(8,128)S(1)}, u32[]{:S(2)}, u32[]{:S(2)}) collective-permute-start(f32[8,64,128]{2,1,0:T(8,128)} %slice.98), channel_id=1, source_target_pairs={{0,1},{1,2},{2,3},{3,4},{4,5},{5,6},{6,7},{7,8},{8,9},{9,10},{10,1... | collective-permute-start | bytes 786440 | tf_op jit(solution)/shard_map/ppermute | solution.py:15
  30.4 5.5 copy-start.14
  30.4 7.1 copy-start.12
  67.8 537.3 %copy-start = (f32[8,512,128]{2,1,0:T(8,128)}, f32[8,512,128]{2,1,0:T(8,128)S(1)}, u32[]{:S(2)}) copy-start(f32[8,512,128]{2,1,0:T(8,128)S(1)} %fusion.21) | copy-start | bytes 6291460
  67.8 2.8 copy-start.7
  71.9 62.0 %all-to-all-start = ((f32[32,32,128]{2,1,0:T(8,128)}), f32[32,32,128]{2,1,0:T(8,128)S(1)}, u32[]{:S(2)}, u32[]{:S(2)}) async-start(f32[32,32,128]{2,1,0:T(8,128)} %get-tuple-element.53), calls=%async_computation | async-start | bytes 1048576 | tf_op jit(solution)/shard_map/all_to_all | solution.py:97
  77.7 213.8 %all-gather.4.cloned.1.call-start = ((), (), s32[]{:S(2)}) async-start(), calls=%async_computation.7 | async-start | bytes 18874368 | tf_op jit(solution)/shard_map/all_gather | solution.py:125
  133.8 1.2 copy-start.13
  139.8 223.7 %all-reduce.6.cloned.1.call-start = ((), (), s32[]{:S(2)}) async-start(), calls=%async_computation.8 | async-start | bytes 2097152 | tf_op jit(solution)/shard_map/psum | solution.py:20
  304.9 1.3 copy-start.5
  306.3 1.2 copy-start.8
  307.3 254.5 %all-gather.6.cloned.1.call-start = ((), (), s32[]{:S(2)}) async-start(), calls=%async_computation.9 | async-start | bytes 18874368 | tf_op jit(solution)/shard_map/all_gather | solution.py:125
  575.3 1.3 copy-start.2
  601.7 19.9 %all-to-all-start.5 = ((f32[32,32,128]{2,1,0:T(8,128)}), f32[32,32,128]{2,1,0:T(8,128)}, u32[]{:S(2)}, u32[]{:S(2)}) async-start(f32[32,32,128]{2,1,0:T(8,128)} %get-tuple-element.50), calls=%async_computation.5 | async-start | bytes 1048576 | tf_op jit(solution)/shard_map/all_to_all | solution.py:100
  605.0 78.4 %all-reduce.8.cloned.1.call-start = ((), (), s32[]{:S(2)}) async-start(), calls=%async_computation.10 | async-start | bytes 2097152 | tf_op jit(solution)/shard_map/psum | solution.py:20
  605.1 10.2 %copy-start.3 = (f32[4096,128]{0,1:T(8,128)S(1)}, f32[4096,128]{0,1:T(8,128)}, u32[]{:S(2)}) copy-start(f32[4096,128]{0,1:T(8,128)} %copy-done.2) | copy-start | bytes 6291460
  605.1 3.2 collective-permute-start.1
  646.7 79.1 %all-to-all-start.4 = ((f32[32,32,128]{2,1,0:T(8,128)}), f32[32,32,128]{2,1,0:T(8,128)S(1)}, u32[]{:S(2)}, u32[]{:S(2)}) async-start(f32[32,32,128]{2,1,0:T(8,128)} %broadcast_select_fusion.2), calls=%async_computation.4 | async-start | bytes 1048576 | tf_op jit(solution)/shard_map/all_to_all | solution.py:97
  657.9 227.9 %all-gather.8.cloned.1.call-start = ((), (), s32[]{:S(2)}) async-start(), calls=%async_computation.11 | async-start | bytes 18874368 | tf_op jit(solution)/shard_map/all_gather | solution.py:125
  740.2 13.5 %collective-permute-start.2 = (f32[8,64,128]{2,1,0:T(8,128)S(1)}, f32[8,64,128]{2,1,0:T(8,128)S(1)}, u32[]{:S(2)}, u32[]{:S(2)}) collective-permute-start(f32[8,64,128]{2,1,0:T(8,128)S(1)} %slice.133), channel_id=1, source_target_pairs={{0,1},{1,2},{2,3},{3,4},{4,5},{5,6},{6,7},{7,8},{8,9},{9,10},{10,1... | collective-permute-start | bytes 786440 | tf_op jit(solution)/shard_map/ppermute | solution.py:15
  894.0 3.1 copy-start.4
Sparse Core Ops, SparseCore 0:
  33.0 58.5 all-reduce.3
  139.9 151.4 all-gather.3
  307.5 56.0 all-reduce.5
  410.7 151.0 all-gather.5
  616.6 66.8 all-reduce.7
  731.9 153.8 all-gather.7
